TPU v7x, 32 devices: a whole 2x2x4 slice. The times are simulated.
32 devices in a mesh: row: 4 (over y, x), col: 8 (over z, core).
Axes of the slice: x: 2, y: 2, z: 4, core: 2. Of those that a mesh axis runs over, the one named last changes fastest.
Arguments:
- pivot: float32 [1024, 1024], replicated, may hold values from -1 to 2
- col_panel: float32 [2048, 1024], P('row', 'col'), may hold values from -0.25 to 0.25
- row_panel: float32 [1024, 2048], P('row', 'col'), may hold values from -6 to 6
- trailing: float32 [2048, 2048], P('row', 'col'), may hold values from -6 to 6
Outputs:
- updated: float32 [2048, 2048], P('row', 'col')
All inputs are finite; a program needn't handle non-finite values.
Results may differ from a plain program's by a relative error of at most 0.000061.
Values sent between devices are 32-bit elements; how exact they have to be, the bound alone decides.
No kernel may reach another device: no remote copies, remote signals or barrier semaphores. Data moves between devices by JAX's collectives and lax.ppermute only.
A program may use at most 64 MiB of HBM per device.

v0:
```python
import jax
import jax.numpy as jnp
from jax import lax
from jax.sharding import PartitionSpec as P

B = 512


def product(left, right):
    return jnp.dot(left, right, precision=lax.Precision.HIGHEST, preferred_element_type=jnp.float32)


def newton_inverse(matrix):
    identity = jnp.eye(matrix.shape[0], dtype=jnp.float32)
    initial = 2.0 * identity - matrix
    return product(initial, 2.0 * identity - product(matrix, initial))


def local(pivot, col_panel, row_panel, trailing):
    gathered_cols = lax.all_gather(col_panel, "col", axis=1, tiled=True)
    gathered_rows = lax.all_gather(row_panel, "row", axis=0, tiled=True)
    top_left = pivot[:B, :B]
    top_right = pivot[:B, B:]
    low_left = pivot[B:, :B]
    low_right = pivot[B:, B:]
    inverse_one = newton_inverse(top_left)
    multiplier = product(low_left, inverse_one)
    schur = low_right - product(multiplier, top_right)
    inverse_two = newton_inverse(schur)
    factor_one = product(gathered_cols[:, :B], inverse_one)
    factor_two = product(gathered_cols[:, B:] - product(factor_one, top_right), inverse_two)
    first_rows = gathered_rows[:B]
    rows_two = gathered_rows[B:] - product(multiplier, first_rows)
    return trailing - product(factor_one, first_rows) - product(factor_two, rows_two)


def solution(mesh):
    return jax.shard_map(
        local,
        mesh=mesh,
        in_specs=(P(), P("row", "col"), P("row", "col"), P("row", "col")),
        out_specs=P("row", "col"),
        check_vma=False,
    )
```

profile of v0, /device:TPU:9, one launch (start us, length us, event | category | flops | bytes accessed | tf_op | source)
XLA Modules:
  0.0 91.9 jit_solution(5261622955538227202)
XLA Ops:
  6.5 0.0 all-gather.5.cloned.1.call-start
  6.5 0.7 all-gather.5.cloned.1.call-update
  7.3 0.0 all-gather.3.cloned.1.call-start
  7.3 0.7 all-gather.3.cloned.1.call-update
  8.0 0.0 copy-start
  8.0 3.7 %select_subtract_fusion.2 = f32[512,512]{1,0:T(8,128)S(1)} fusion(f32[1024,1024]{1,0:T(8,128)} %param.4), kind=kOutput, calls=%fused_computation.2 | convolution fusion | flops 1612185600 | bytes 3145728 | tf_op jit(solution)/shard_map/dot_general | solution.py:10
  11.7 3.1 %fusion = f32[512,512]{1,0:T(8,128)S(1)} fusion(f32[512,512]{1,0:T(8,128)S(1)} %select_subtract_fusion.2, f32[1024,1024]{1,0:T(8,128)} %param.4), kind=kOutput, calls=%fused_computation.7 | convolution fusion | flops 1611399168 | bytes 3145728 | tf_op jit(solution)/shard_map/dot_general | solution.py:10
  14.9 0.0 copy-done
  14.9 3.5 %fusion.4 = f32[512,512]{1,0:T(8,128)S(1)} fusion(f32[512,512]{1,0:T(8,128)S(1)} %fusion, f32[1024,1024]{1,0:T(8,128)S(1)} %copy-done), kind=kOutput, calls=%fused_computation.14 | convolution fusion | flops 1610612736 | bytes 3145728 | tf_op jit(solution)/shard_map/dot_general | solution.py:10
  18.3 1.8 %convolution_subtract_fusion = f32[512,512]{1,0:T(8,128)S(1)} fusion(f32[512,512]{1,0:T(8,128)S(1)} %fusion.4, f32[1024,1024]{1,0:T(8,128)S(1)} %copy-done), kind=kOutput, calls=%fused_computation.4 | convolution fusion | flops 1610874880 | bytes 4194304 | tf_op jit(solution)/shard_map/dot_general | solution.py:10
  20.2 1.9 %select_subtract_fusion = f32[512,512]{1,0:T(8,128)S(1)} fusion(f32[512,512]{1,0:T(8,128)S(1)} %convolution_subtract_fusion), kind=kOutput, calls=%fused_computation | convolution fusion | flops 1612185600 | bytes 2097152 | tf_op jit(solution)/shard_map/dot_general | solution.py:10
  22.1 2.1 %fusion.1 = f32[512,512]{1,0:T(8,128)S(1)} fusion(f32[512,512]{1,0:T(8,128)S(1)} %select_subtract_fusion, f32[512,512]{1,0:T(8,128)S(1)} %convolution_subtract_fusion), kind=kOutput, calls=%fused_computation.8 | convolution fusion | flops 1611399168 | bytes 3145728 | tf_op jit(solution)/shard_map/dot_general | solution.py:10
  24.2 12.5 %all-gather.5.cloned.1.call-done = f32[1024,256]{1,0:T(8,128)} async-done(((f32[256,256]{1,0:T(8,128)}), f32[1024,256]{1,0:T(8,128)}) %all-gather.5.cloned.1.call-update) | async-done | bytes 1048592 | tf_op jit(solution)/shard_map/all_gather | solution.py:21
  36.7 3.8 %convolution_subtract_fusion.3 = f32[512,256]{1,0:T(8,128)} fusion(f32[512,512]{1,0:T(8,128)S(1)} %fusion.4, f32[1024,256]{1,0:T(8,128)} %all-gather.5.cloned.1.call-done), kind=kOutput, calls=%fused_computation.10 | convolution fusion | flops 805437440 | bytes 2621440 | tf_op jit(solution)/shard_map/dot_general | solution.py:10
  40.5 30.8 %all-gather.3.cloned.1.call-done = f32[512,1024]{1,0:T(8,128)} async-done(((f32[512,128]{1,0:T(8,128)}), f32[512,1024]{1,0:T(8,128)}) %all-gather.3.cloned.1.call-update) | async-done | bytes 2097168 | tf_op jit(solution)/shard_map/all_gather | solution.py:20
  71.3 4.7 %fusion.2 = f32[512,512]{1,0:T(8,128)S(1)} fusion(f32[512,512]{1,0:T(8,128)S(1)} %fusion, f32[512,1024]{1,0:T(8,128)} %all-gather.3.cloned.1.call-done), kind=kOutput, calls=%fused_computation.12 | convolution fusion | flops 1610612736 | bytes 3145728 | tf_op jit(solution)/shard_map/dot_general | solution.py:10
  76.0 0.0 copy-start.2
  76.0 0.0 copy-start.3
  76.0 0.0 copy-start.1
  76.0 3.5 %convolution_subtract_fusion.1 = f32[512,512]{1,0:T(8,128)S(1)} fusion(f32[512,512]{1,0:T(8,128)S(1)} %fusion.2, f32[512,1024]{1,0:T(8,128)} %all-gather.3.cloned.1.call-done, f32[1024,1024]{1,0:T(8,128)} %param.4), kind=kOutput, calls=%fused_computation.5 | convolution fusion | flops 1610874880 | bytes 4194304 | tf_op jit(solution)/shard_map/dot_general | solution.py:10
  79.5 1.8 %fusion.28 = f32[512,512]{1,0:T(8,128)S(1)} fusion(f32[512,512]{1,0:T(8,128)S(1)} %convolution_subtract_fusion.1, f32[512,512]{1,0:T(8,128)S(1)} %fusion.1), kind=kOutput, calls=%fused_computation.39 | convolution fusion | flops 1610612736 | bytes 3145728 | tf_op jit(solution)/shard_map/dot_general | solution.py:10
  81.4 0.0 copy-done.2
  81.4 0.0 copy-done.3
  81.4 1.8 %convolution_subtract_fusion.4 = f32[512,256]{1,0:T(8,128)S(1)} fusion(f32[512,256]{1,0:T(8,128)S(1)} %copy-done.3, f32[512,512]{1,0:T(8,128)S(1)} %fusion.2, f32[1024,256]{1,0:T(8,128)S(1)} %copy-done.2), kind=kOutput, calls=%fused_computation.11 | convolution fusion | flops 805437440 | bytes 2621440 | tf_op jit(solution)/shard_map/dot_general | solution.py:10
  83.2 0.0 copy-done.1
  83.2 1.8 %convolution_subtract_fusion.2 = f32[512,256]{1,0:T(8,128)} fusion(f32[512,256]{1,0:T(8,128)S(1)} %convolution_subtract_fusion.4, f32[512,512]{1,0:T(8,128)S(1)} %fusion.28, f32[512,256]{1,0:T(8,128)S(1)} %copy-done.1), kind=kOutput, calls=%fused_computation.9 | convolution fusion | flops 805437440 | bytes 2621440 | tf_op jit(solution)/shard_map/dot_general | solution.py:10
Async XLA Ops:
  6.5 30.2 %all-gather.5.cloned.1.call-start = ((), (), s32[]{:S(2)}) async-start(), calls=%async_computation.1 | async-start | bytes 1310720 | tf_op jit(solution)/shard_map/all_gather | solution.py:21
  7.3 64.0 %all-gather.3.cloned.1.call-start = ((), (), s32[]{:S(2)}) async-start(), calls=%async_computation | async-start | bytes 2359296 | tf_op jit(solution)/shard_map/all_gather | solution.py:20
  8.0 6.9 %copy-start = (f32[1024,1024]{1,0:T(8,128)S(1)}, f32[1024,1024]{1,0:T(8,128)}, u32[]{:S(2)}) copy-start(f32[1024,1024]{1,0:T(8,128)} %param.4) | copy-start | bytes 12582916
  76.0 5.4 %copy-start.2 = (f32[1024,256]{1,0:T(8,128)S(1)}, f32[1024,256]{1,0:T(8,128)}, u32[]{:S(2)}) copy-start(f32[1024,256]{1,0:T(8,128)} %all-gather.5.cloned.1.call-done) | copy-start | bytes 3145732
  76.0 5.4 %copy-start.3 = (f32[512,256]{1,0:T(8,128)S(1)}, f32[512,256]{1,0:T(8,128)}, u32[]{:S(2)}) copy-start(f32[512,256]{1,0:T(8,128)} %param.7) | copy-start | bytes 1572868
  76.0 7.3 %copy-start.1 = (f32[512,256]{1,0:T(8,128)S(1)}, f32[512,256]{1,0:T(8,128)}, u32[]{:S(2)}) copy-start(f32[512,256]{1,0:T(8,128)} %convolution_subtract_fusion.3) | copy-start | bytes 1572868
Sparse Core Ops, SparseCore 0:
  9.2 27.4 all-gather.4
  38.3 32.9 all-gather.2
where the time goes:
time: 92.1 us; the launch traced here: 91.9 us
  waiting for transfers between devices  44.7 us (49%)
  matrix products  33.6 us (36%)
  between operations  13.5 us (15%)
    dot_general x12, matrix products, product(): jnp.dot(left, right, precision=lax.Precision.HIGHEST, preferred_element_t...  33.6 us
    all_gather x1, waiting for transfers between devices, local(): gathered_cols = lax.all_gather(col_panel, 'col', axis=1, tiled=True)  30.8 us
    all_gather x1, waiting for transfers between devices, local(): gathered_rows = lax.all_gather(row_panel, 'row', axis=0, tiled=True)  12.5 us
  transfers between devices with their start and end apart: 2, of which 2 were waited for; matrix products, arithmetic and copies ran while one was open for 22% of the time, Pallas kernels for 0%

commit v1 on v0

--- a/solution.py
+++ b/solution.py
@@ -4,6 +4,17 @@
 from jax.sharding import PartitionSpec as P
 
 B = 512
+
+
+def around_the_ring(value, name, d):
+    n_dev = lax.axis_size(name)
+    right = [(i, (i + 1) % n_dev) for i in range(n_dev)]
+    terms = [value]
+    for reach in range(1, n_dev):
+        terms = [lax.ppermute(terms[0], name, right), *terms]
+    out = jnp.concatenate(terms, axis=d)
+    offset = (lax.axis_index(name) + 1) * terms[-1].shape[d]
+    return jnp.roll(out, offset, axis=d)
 
 
 def product(left, right):
@@ -18,7 +29,7 @@
 
 def local(pivot, col_panel, row_panel, trailing):
     gathered_cols = lax.all_gather(col_panel, "col", axis=1, tiled=True)
-    gathered_rows = lax.all_gather(row_panel, "row", axis=0, tiled=True)
+    gathered_rows = around_the_ring(row_panel, "row", 0)
     top_left = pivot[:B, :B]
     top_right = pivot[:B, B:]
     low_left = pivot[B:, :B]

time: 92.1 us -> 63.3 us (0.69)
  waiting for transfers between devices: 44.7 us -> 13.9 us
  starting transfers between devices: 0.04 us -> 2.94 us
  matrix products: 33.6 us -> 31.1 us
  local copies, waits for them, and re-layouts: 0.02 us -> 1.51 us
    all_gather x1, waiting for transfers between devices: 30.8 us -> 3.79 us  [local(): gathered_cols = lax.all_gather(col_panel, 'col', axis=1, tiled=True)]
    all_gather x1 -> x0, waiting for transfers between devices: 12.5 us -> none  [local(): gathered_rows = lax.all_gather(row_panel, 'row', axis=0, tiled=True)]
    ppermute x0 -> x3, waiting for transfers between devices: none -> 9.45 us  [around_the_ring(): terms = [lax.ppermute(terms[0], name, right), *terms]]
    ppermute x0 -> x3, starting transfers between devices: none -> 2.94 us  [around_the_ring(): terms = [lax.ppermute(terms[0], name, right), *terms]]
    dot_general x12, matrix products: 33.6 us -> 31.1 us  [product(): jnp.dot(left, right, precision=lax.Precision.HIGHEST, preferred_element_t...]
    unnamed x8 -> x19, local copies, waits for them, and re-layouts: 0.02 us -> 1.49 us
  transfers between devices with their start and end apart: 2 -> 4, of which waited for: 2 -> 3; matrix products, arithmetic and copies ran while one was open for 22% -> 28% of each run, Pallas kernels for 0% -> 0%
where the time goes in v1:
time: 63.3 us; the launch traced here: 63.1 us
  matrix products  31.1 us (49%)
  waiting for transfers between devices  13.9 us (22%)
  between operations  13.6 us (21%)
  starting transfers between devices  2.94 us (5%)
  local copies, waits for them, and re-layouts  1.51 us (2%)
    dot_general x12, matrix products, product(): jnp.dot(left, right, precision=lax.Precision.HIGHEST, preferred_element_t...  31.1 us
    ppermute x3, waiting for transfers between devices, around_the_ring(): terms = [lax.ppermute(terms[0], name, right), *terms]  9.45 us
    all_gather x1, waiting for transfers between devices, local(): gathered_cols = lax.all_gather(col_panel, 'col', axis=1, tiled=True)  3.79 us
    ppermute x3, starting transfers between devices, around_the_ring(): terms = [lax.ppermute(terms[0], name, right), *terms]  2.94 us
    unnamed x19, local copies, waits for them, and re-layouts  1.49 us
  transfers between devices with their start and end apart: 4, of which 3 were waited for; matrix products, arithmetic and copies ran while one was open for 28% of the time, Pallas kernels for 0%

profile of v1, /device:TPU:9, one launch (start us, length us, event | category | flops | bytes accessed | tf_op | source)
XLA Modules:
  0.0 63.1 jit_solution(11164768355471604542)
XLA Ops:
  6.5 0.0 all-gather.2.cloned.1.call-start
  6.5 0.7 %all-gather.2.cloned.1.call-update = ((f32[512,128]{1,0:T(8,128)}), f32[512,1024]{1,0:T(8,128)}) async-update(((), (), s32[]{:S(2)}) %all-gather.2.cloned.1.call-start, f32[512,128]{1,0:T(8,128)} %param.5) | async-update | bytes 2621464
  7.3 1.3 %collective-permute-start = (f32[256,256]{1,0:T(8,128)}, f32[256,256]{1,0:T(8,128)S(1)}, u32[]{:S(2)}, u32[]{:S(2)}) collective-permute-start(f32[256,256]{1,0:T(8,128)} %param.6), channel_id=1, source_target_pairs={{0,8},{8,16},{16,24},{24,0},{1,9},{9,17},{17,25},{25,1},{2,10},{10... | collective-permute-start | bytes 786440 | tf_op jit(solution)/shard_map/ppermute | solution.py:14
  8.5 0.0 copy-start
  8.5 3.7 %select_subtract_fusion.2 = f32[512,512]{1,0:T(8,128)S(1)} fusion(f32[1024,1024]{1,0:T(8,128)} %param.4), kind=kOutput, calls=%fused_computation.2 | convolution fusion | flops 1612185600 | bytes 3145728 | tf_op jit(solution)/shard_map/dot_general | solution.py:21
  12.2 3.1 %fusion = f32[512,512]{1,0:T(8,128)S(1)} fusion(f32[512,512]{1,0:T(8,128)S(1)} %select_subtract_fusion.2, f32[1024,1024]{1,0:T(8,128)} %param.4), kind=kOutput, calls=%fused_computation.7 | convolution fusion | flops 1611399168 | bytes 3145728 | tf_op jit(solution)/shard_map/dot_general | solution.py:21
  15.4 0.0 copy-done
  15.4 3.5 %fusion.5 = f32[512,512]{1,0:T(8,128)S(1)} fusion(f32[512,512]{1,0:T(8,128)S(1)} %fusion, f32[1024,1024]{1,0:T(8,128)S(1)} %copy-done), kind=kOutput, calls=%fused_computation.13 | convolution fusion | flops 1610612736 | bytes 3145728 | tf_op jit(solution)/shard_map/dot_general | solution.py:21
  18.9 1.8 %convolution_subtract_fusion = f32[512,512]{1,0:T(8,128)S(1)} fusion(f32[512,512]{1,0:T(8,128)S(1)} %fusion.5, f32[1024,1024]{1,0:T(8,128)S(1)} %copy-done), kind=kOutput, calls=%fused_computation.4 | convolution fusion | flops 1610874880 | bytes 4194304 | tf_op jit(solution)/shard_map/dot_general | solution.py:21
  20.7 0.0 collective-permute-done
  20.7 1.3 %collective-permute-start.1 = (f32[256,256]{1,0:T(8,128)S(1)}, f32[256,256]{1,0:T(8,128)S(1)}, u32[]{:S(2)}, u32[]{:S(2)}) collective-permute-start(f32[256,256]{1,0:T(8,128)S(1)} %collective-permute-done), channel_id=1, source_target_pairs={{0,8},{8,16},{16,24},{24,0},{1,9},{9,17},{17,25},{25,1},{2,10},{10... | collective-permute-start | bytes 786440 | tf_op jit(solution)/shard_map/ppermute | solution.py:14
  22.0 1.9 %select_subtract_fusion = f32[512,512]{1,0:T(8,128)S(1)} fusion(f32[512,512]{1,0:T(8,128)S(1)} %convolution_subtract_fusion), kind=kOutput, calls=%fused_computation | convolution fusion | flops 1612185600 | bytes 2097152 | tf_op jit(solution)/shard_map/dot_general | solution.py:21
  23.9 0.0 copy-start.4
  23.9 4.7 %collective-permute-done.1 = f32[256,256]{1,0:T(8,128)S(1)} collective-permute-done((f32[256,256]{1,0:T(8,128)S(1)}, f32[256,256]{1,0:T(8,128)S(1)}, u32[]{:S(2)}, u32[]{:S(2)}) %collective-permute-start.1) | collective-permute-done | bytes 262176 | tf_op jit(solution)/shard_map/ppermute | solution.py:14
  28.6 0.4 collective-permute-start.2
  29.0 1.9 %fusion.1 = f32[512,512]{1,0:T(8,128)S(1)} fusion(f32[512,512]{1,0:T(8,128)S(1)} %select_subtract_fusion, f32[512,512]{1,0:T(8,128)S(1)} %convolution_subtract_fusion), kind=kOutput, calls=%fused_computation.8 | convolution fusion | flops 1611399168 | bytes 3145728 | tf_op jit(solution)/shard_map/dot_general | solution.py:21
  30.9 4.8 %collective-permute-done.2 = f32[256,256]{1,0:T(8,128)S(1)} collective-permute-done((f32[256,256]{1,0:T(8,128)S(1)}, f32[256,256]{1,0:T(8,128)S(1)}, u32[]{:S(2)}, u32[]{:S(2)}) %collective-permute-start.2) | collective-permute-done | bytes 262176 | tf_op jit(solution)/shard_map/ppermute | solution.py:14
  35.7 0.0 copy-done.4
  35.9 0.0 copy-start.2
  35.9 1.3 %copy-done.2 = f32[2048,256]{1,0:T(8,128)} copy-done((f32[2048,256]{1,0:T(8,128)}, f32[2048,256]{1,0:T(8,128)S(1)}, u32[]{:S(2)}) %copy-start.2) | copy-done | bytes 2097176
  37.2 1.8 %fusion.20 = f32[512,256]{1,0:T(8,128)S(1)} fusion(f32[512,512]{1,0:T(8,128)S(1)} %fusion.5, f32[2048,256]{1,0:T(8,128)S(1)} %constant_dynamic-update-slice_fusion, s32[]{:T(128)S(6)} %select_n.14), kind=kOutput, calls=%fused_computation.30 | convolution fusion | flops 805306368 | bytes 2097156 | tf_op jit(solution)/shard_map/dot_general | solution.py:21
  39.0 3.8 %all-gather.2.cloned.1.call-done = f32[512,1024]{1,0:T(8,128)} async-done(((f32[512,128]{1,0:T(8,128)}), f32[512,1024]{1,0:T(8,128)}) %all-gather.2.cloned.1.call-update) | async-done | bytes 2097168 | tf_op jit(solution)/shard_map/all_gather | solution.py:31
  42.8 0.0 copy-start.1
  42.8 4.8 %fusion.3 = f32[512,512]{1,0:T(8,128)S(1)} fusion(f32[512,512]{1,0:T(8,128)S(1)} %fusion, f32[512,1024]{1,0:T(8,128)} %all-gather.2.cloned.1.call-done), kind=kOutput, calls=%fused_computation.11 | convolution fusion | flops 1610612736 | bytes 3145728 | tf_op jit(solution)/shard_map/dot_general | solution.py:21
  47.6 0.0 copy-done.1
  47.7 3.1 %convolution_subtract_fusion.1 = f32[512,512]{1,0:T(8,128)S(1)} fusion(f32[512,512]{1,0:T(8,128)S(1)} %fusion.3, f32[512,1024]{1,0:T(8,128)S(1)} %copy-done.1, f32[1024,1024]{1,0:T(8,128)} %param.4), kind=kOutput, calls=%fused_computation.5 | convolution fusion | flops 1610874880 | bytes 4194304 | tf_op jit(solution)/shard_map/dot_general | solution.py:21
  50.7 0.0 copy-start.3
  50.7 1.8 %fusion.34 = f32[512,512]{1,0:T(8,128)S(1)} fusion(f32[512,512]{1,0:T(8,128)S(1)} %convolution_subtract_fusion.1, f32[512,512]{1,0:T(8,128)S(1)} %fusion.1), kind=kOutput, calls=%fused_computation.52 | convolution fusion | flops 1610612736 | bytes 3145728 | tf_op jit(solution)/shard_map/dot_general | solution.py:21
  52.6 0.0 copy-done.3
  52.6 0.0 copy-start.5
  52.6 1.0 %fusion.11 = f32[512,256]{1,0:T(8,128)S(1)} fusion(f32[512,512]{1,0:T(8,128)S(1)} %fusion.34, f32[512,256]{1,0:T(8,128)S(1)} %fusion.20, f32[2048,256]{1,0:T(8,128)S(1)} %copy-done.3, s32[]{:T(128)S(6)} %add.16), kind=kOutput, calls=%fused_computation.21 | convolution fusion | flops 805437440 | bytes 2621444 | tf_op jit(solution)/shard_map/dot_general | solution.py:21
  53.6 0.0 copy-done.5
  53.7 2.6 %fusion.2 = f32[512,256]{1,0:T(8,128)} fusion(f32[512,256]{1,0:T(8,128)S(1)} %fusion.11, f32[512,256]{1,0:T(8,128)S(1)} %copy-done.5, f32[512,512]{1,0:T(8,128)S(1)} %fusion.3, f32[2048,256]{1,0:T(8,128)S(1)} %copy-done.3, s32[]{:T(128)S(6)} %select_n.14), kind=kOutput, calls=%fused_computation.10 | convolution fusion | flops 805568512 | bytes 3145732 | tf_op jit(solution)/shard_map/dot_general | solution.py:21
  (8 shorter events, 0.2 us)
Async XLA Ops:
  6.5 36.3 %all-gather.2.cloned.1.call-start = ((), (), s32[]{:S(2)}) async-start(), calls=%async_computation | async-start | bytes 2359296 | tf_op jit(solution)/shard_map/all_gather | solution.py:31
  7.3 13.5 %collective-permute-start = (f32[256,256]{1,0:T(8,128)}, f32[256,256]{1,0:T(8,128)S(1)}, u32[]{:S(2)}, u32[]{:S(2)}) collective-permute-start(f32[256,256]{1,0:T(8,128)} %param.6), channel_id=1, source_target_pairs={{0,8},{8,16},{16,24},{24,0},{1,9},{9,17},{17,25},{25,1},{2,10},{10... | collective-permute-start | bytes 786440 | tf_op jit(solution)/shard_map/ppermute | solution.py:14
  8.5 6.8 %copy-start = (f32[1024,1024]{1,0:T(8,128)S(1)}, f32[1024,1024]{1,0:T(8,128)}, u32[]{:S(2)}) copy-start(f32[1024,1024]{1,0:T(8,128)} %param.4) | copy-start | bytes 12582916
  20.7 7.9 %collective-permute-start.1 = (f32[256,256]{1,0:T(8,128)S(1)}, f32[256,256]{1,0:T(8,128)S(1)}, u32[]{:S(2)}, u32[]{:S(2)}) collective-permute-start(f32[256,256]{1,0:T(8,128)S(1)} %collective-permute-done), channel_id=1, source_target_pairs={{0,8},{8,16},{16,24},{24,0},{1,9},{9,17},{17,25},{25,1},{2,10},{10... | collective-permute-start | bytes 786440 | tf_op jit(solution)/shard_map/ppermute | solution.py:14
  23.9 11.8 %copy-start.4 = (f32[256,256]{1,0:T(8,128)S(1)}, f32[256,256]{1,0:T(8,128)}, u32[]{:S(2)}) copy-start(f32[256,256]{1,0:T(8,128)} %param.6) | copy-start | bytes 786436
  28.6 7.1 %collective-permute-start.2 = (f32[256,256]{1,0:T(8,128)S(1)}, f32[256,256]{1,0:T(8,128)S(1)}, u32[]{:S(2)}, u32[]{:S(2)}) collective-permute-start(f32[256,256]{1,0:T(8,128)S(1)} %collective-permute-done.1), channel_id=1, source_target_pairs={{0,8},{8,16},{16,24},{24,0},{1,9},{9,17},{17,25},{25,1},{2,10},{10... | collective-permute-start | bytes 786440 | tf_op jit(solution)/shard_map/ppermute | solution.py:14
  35.9 1.3 %copy-start.2 = (f32[2048,256]{1,0:T(8,128)}, f32[2048,256]{1,0:T(8,128)S(1)}, u32[]{:S(2)}) copy-start(f32[2048,256]{1,0:T(8,128)S(1)} %constant_dynamic-update-slice_fusion) | copy-start | bytes 6291460
  42.8 4.9 %copy-start.1 = (f32[512,1024]{1,0:T(8,128)S(1)}, f32[512,1024]{1,0:T(8,128)}, u32[]{:S(2)}) copy-start(f32[512,1024]{1,0:T(8,128)} %all-gather.2.cloned.1.call-done) | copy-start | bytes 6291460
  50.7 1.9 %copy-start.3 = (f32[2048,256]{1,0:T(8,128)S(1)}, f32[2048,256]{1,0:T(8,128)}, u32[]{:S(2)}) copy-start(f32[2048,256]{1,0:T(8,128)} %copy-done.2) | copy-start | bytes 6291460
  52.6 1.0 %copy-start.5 = (f32[512,256]{1,0:T(8,128)S(1)}, f32[512,256]{1,0:T(8,128)}, u32[]{:S(2)}) copy-start(f32[512,256]{1,0:T(8,128)} %param.7) | copy-start | bytes 1572868
Sparse Core Ops, SparseCore 0:
  8.9 33.8 all-gather.1
